TPU v7x, 32 devices: a whole 2x2x4 slice. The times are simulated.
32 devices in a mesh: seq: 32 (over z, y, x, core).
Axes of the slice: x: 2, y: 2, z: 4, core: 2. Of those that a mesh axis runs over, the one named last changes fastest.
Arguments:
- tokens: bfloat16 [5120, 2048], P('seq'), may hold values from -6 to 6
- cotangent: bfloat16 [5120, 2048], P('seq'), may hold values from -6 to 6
- gate_codes: int32 [5120, 256], P('seq'), may hold values from 256 to 4096, as said below
- lengths: int32 [4], replicated, may hold values from 1 to 2560, 5120 in all
- mixer_gain: bfloat16 [2048], P('seq'), may hold values from 0.099609375 to 1.8984375
- query_weight: bfloat16 [2048, 2048], P('seq'), may hold values from -0.125 to 0.125
- key_weight: bfloat16 [2048, 2048], P('seq'), may hold values from -0.125 to 0.125
- value_weight: bfloat16 [2048, 2048], P('seq'), may hold values from -0.125 to 0.125
- head_gain: bfloat16 [2048], P('seq'), may hold values from 0.099609375 to 1.8984375
- output_weight: bfloat16 [2048, 2048], P('seq'), may hold values from -0.125 to 0.125
- feed_gain: bfloat16 [2048], P('seq'), may hold values from 0.099609375 to 1.8984375
- gate_weight: bfloat16 [2048, 5632], P('seq'), may hold values from -0.125 to 0.125
- up_weight: bfloat16 [2048, 5632], P('seq'), may hold values from -0.125 to 0.125
- down_weight: bfloat16 [2048, 5632], P('seq'), may hold values from -0.078125 to 0.078125
Outputs:
- block_out: bfloat16 [5120, 2048], P('seq')
- input_grad: float32 [5120, 2048], P('seq')
- mixer_gain_grad: float32 [2048], P('seq')
- query_grad: float32 [2048, 2048], P('seq')
- key_grad: float32 [2048, 2048], P('seq')
- value_grad: float32 [2048, 2048], P('seq')
- head_gain_grad: float32 [2048], P('seq')
- output_weight_grad: float32 [2048, 2048], P('seq')
- feed_gain_grad: float32 [2048], P('seq')
- gate_grad: float32 [2048, 5632], P('seq')
- up_grad: float32 [2048, 5632], P('seq')
- down_grad: float32 [2048, 5632], P('seq')
Inputs may be any that keep to these rules, and one draw needn't show every extreme that they name: `gate_codes`: whole numbers, forget-gate logits of each token and each of the 4 x 64 slots, times 256. The 4 sequences lie one after another along the tokens; the lengths add up to 5120 and the longest is exactly 2560.
All inputs are finite; a program needn't handle non-finite values.
Results may differ from a plain program's by a relative error of at most 0.017.
The roundings to bfloat16 on the way count: a program that leaves them out, or rounds other values in their place, can miss the bound.
Values may be sent and summed in bfloat16 or wider, within the bound.
A program may use at most 504 MiB of HBM per device.

v0:
```python
import jax
import jax.numpy as jnp
from jax import lax
from jax.sharding import PartitionSpec as P

HEADS = 4
SLOTS = 64
epsilon = 1e-06
highest = lax.Precision.HIGHEST
contract_last = (((1,), (1,)), ((), ()))
contract_first = (((0,), (0,)), ((), ()))


def entering(shard, axis, combine, identity):
    devices, index = (lax.axis_size(axis), lax.axis_index(axis))
    everything = jax.tree.map(lambda part: lax.all_gather(part, axis), shard)
    start = jax.tree.map(
        lambda part, zero: jnp.broadcast_to(jnp.asarray(zero, part.dtype), part.shape),
        shard,
        identity,
    )

    def entering_step(k, before):
        reached = k < index
        new = combine(before, jax.tree.map(lambda part: part[k], everything))
        return jax.tree.map(lambda a, b: jnp.where(reached, a, b), new, before)

    return lax.fori_loop(0, devices, entering_step, start)


def carried_in(shard, axis, combine, identity):
    devices, index = (lax.axis_size(axis), lax.axis_index(axis))
    everything = jax.tree.map(
        lambda part, kind: lax.all_gather(part.astype(kind), axis),
        shard,
        (jnp.bfloat16, jnp.bfloat16),
    )
    start = jax.tree.map(
        lambda part, zero: jnp.broadcast_to(jnp.asarray(zero, part.dtype), part.shape),
        shard,
        identity,
    )

    def carried_step(k, before):
        at = devices - 1 - k
        reached = at > index
        new = combine(
            before, jax.tree.map(lambda part, own: part[at].astype(own.dtype), everything, shard)
        )
        return jax.tree.map(lambda a, b: jnp.where(reached, a, b), new, before)

    return lax.fori_loop(0, devices, carried_step, start)


def rms_factor(value_rows):
    return lax.rsqrt(jnp.mean(value_rows * value_rows, axis=-1, keepdims=True) + epsilon)


def precise_result(form, left, right):
    return jnp.einsum(form, left, right, precision=highest, preferred_element_type=jnp.float32)


def plain_result(form, left, right):
    return jnp.einsum(form, left, right, preferred_element_type=jnp.float32)


def chain_join(earlier, later):
    return (earlier[0] * later[0], later[0][..., None] * earlier[1] + later[1])


def block_tables(decay, starts):
    count = jnp.cumsum(starts)
    length = decay.shape[0]
    places = jnp.arange(length)
    before = places[:, None] >= places[None, :]
    same = jnp.where(before & (count[:, None] == count[None, :]), 1.0, 0.0).astype(jnp.float32)
    fresh_state = jnp.where(count == 0, 1.0, 0.0).astype(jnp.float32)
    logsum = jnp.cumsum(decay, axis=0)
    growth_factor = jnp.exp(logsum)
    backward_pass = jnp.exp(-logsum) * -jnp.expm1(decay)
    tail = jnp.where(count == count[-1], 1.0, 0.0).astype(jnp.float32)
    weight_matrix = growth_factor[-1][None] * backward_pass * tail[:, None, None]
    carried_state = fresh_state[-1] * growth_factor[-1]
    return (same, fresh_state, growth_factor, backward_pass, weight_matrix, carried_state)


def local(
    tokens,
    cotangent,
    gate_codes,
    lengths,
    mixer_gain,
    query_weight,
    key_weight,
    value_weight,
    head_gain,
    output_weight,
    feed_gain,
    gate_weight,
    up_weight,
    down_weight,
):
    local_rows = tokens.shape[0]
    width = tokens.shape[1]
    head_size = width // HEADS
    hidden_width = gate_weight.shape[1]
    tokens_f = tokens.astype(jnp.float32)
    factor_one = rms_factor(tokens_f)
    normed_one = tokens_f * factor_one
    position = lax.axis_index("seq") * local_rows + jnp.arange(local_rows, dtype=jnp.int32)
    first_token = jnp.cumsum(lengths) - lengths
    starts = jnp.sum(jnp.where(position[:, None] == first_token[None, :], 1, 0), axis=1).astype(
        jnp.int32
    )
    decay = jax.nn.log_sigmoid(gate_codes.astype(jnp.float32) / 256.0).reshape(
        local_rows, HEADS, SLOTS
    )
    same, fresh_state, growth_factor, backward_pass, weight_matrix, carried_state = block_tables(
        decay, starts
    )
    piece_a = lax.all_gather(mixer_gain, "seq", axis=0, tiled=True)
    piece_b = lax.all_gather(head_gain, "seq", axis=0, tiled=True)
    piece_c = lax.all_gather(feed_gain, "seq", axis=0, tiled=True)
    piece_query = lax.all_gather(query_weight, "seq", axis=0, tiled=True)
    piece_key = lax.all_gather(key_weight, "seq", axis=0, tiled=True)
    piece_value = lax.all_gather(value_weight, "seq", axis=0, tiled=True)
    section = (normed_one * piece_a.astype(jnp.float32)[None, :]).astype(jnp.bfloat16)
    normed_b = section
    query_acc = jnp.dot(section, piece_query, preferred_element_type=jnp.float32)
    key_acc = jnp.dot(section, piece_key, preferred_element_type=jnp.float32)
    value_acc = jnp.dot(section, piece_value, preferred_element_type=jnp.float32)
    heads_shape = (local_rows, HEADS, head_size)
    query_rows = query_acc.astype(jnp.bfloat16).reshape(heads_shape)
    key_rows = key_acc.astype(jnp.bfloat16).reshape(heads_shape)
    value_rows = value_acc.astype(jnp.bfloat16).reshape(heads_shape)
    query_float = query_rows.astype(jnp.float32)
    local_state = jnp.concatenate(
        [
            precise_result("oft,ofi->fti", weight_matrix, key_rows.astype(jnp.float32)),
            precise_result("oft,ofi->fti", weight_matrix, value_rows.astype(jnp.float32)),
        ],
        axis=-1,
    )
    unit = jnp.ones_like(carried_state)
    blank = jnp.zeros_like(local_state)
    gain_in, state_in = entering((carried_state, local_state), "seq", chain_join, (unit, blank))
    running_key_state = state_in[..., :head_size]
    running_value_state = state_in[..., head_size:]
    affinity = plain_result("thd,shd->hts", query_rows, key_rows)
    masked_scores = affinity * same[None]
    score_matrix = growth_factor * precise_result(
        "ynf,fye->nye", masked_scores, backward_pass
    ) + growth_factor * fresh_state[:, None, None] * precise_result(
        "egr,gjr->egj", query_float, running_key_state
    )
    probs = jax.nn.softmax(score_matrix, axis=-1)
    lifted = probs * growth_factor
    mixing_matrix = (precise_result("thm,shm->hts", lifted, backward_pass) * same[None]).astype(
        jnp.bfloat16
    )
    entry_point = lifted * fresh_state[:, None, None]
    slot_output = plain_result("via,avj->ivj", mixing_matrix, value_rows) + precise_result(
        "xfj,fjg->xfg", entry_point, running_value_state
    )
    head_factor = rms_factor(slot_output)
    unit_heads = slot_output * head_factor
    head_gain_f = piece_b.astype(jnp.float32).reshape(HEADS, head_size)
    normed_heads = (unit_heads * head_gain_f).astype(jnp.bfloat16).reshape(local_rows, width)
    mixed = jnp.dot(
        normed_heads,
        lax.all_gather(output_weight, "seq", axis=0, tiled=True),
        preferred_element_type=jnp.float32,
    )
    residual = tokens_f + mixed
    factor_two = rms_factor(residual)
    normed_two = residual * factor_two
    feed_input = (normed_two * piece_c.astype(jnp.float32)).astype(jnp.bfloat16)
    pieces = (
        lax.all_gather(gate_weight, "seq", axis=0, tiled=True),
        lax.all_gather(up_weight, "seq", axis=0, tiled=True),
    )
    section = feed_input
    gate = jnp.dot(section, pieces[0], preferred_element_type=jnp.float32)
    upward = jnp.dot(section, pieces[1], preferred_element_type=jnp.float32)
    sigma = jax.nn.sigmoid(gate)
    active = gate * sigma
    hidden = (active * upward).astype(jnp.bfloat16)
    feed_out = lax.dot_general(
        hidden,
        lax.all_gather(down_weight, "seq", axis=0, tiled=True),
        contract_last,
        preferred_element_type=jnp.float32,
    )
    block_out = (residual + feed_out).astype(jnp.bfloat16)
    cotangent_f = cotangent.astype(jnp.float32)
    hidden_grad = jnp.dot(
        cotangent,
        lax.all_gather(down_weight, "seq", axis=0, tiled=True),
        preferred_element_type=jnp.float32,
    )
    gate_back = (hidden_grad * upward * sigma * (1.0 + gate * (1.0 - sigma))).astype(jnp.bfloat16)
    up_back = (hidden_grad * active).astype(jnp.bfloat16)
    pieces = lax.all_gather((gate_weight, up_weight), "seq", axis=0, tiled=True)
    feed_in_grad = lax.dot_general(
        gate_back, pieces[0], contract_last, preferred_element_type=jnp.float32
    ) + lax.dot_general(up_back, pieces[1], contract_last, preferred_element_type=jnp.float32)
    feed_grads = jnp.concatenate([gate_back, up_back], axis=1)
    feed_sums = lax.psum_scatter(
        jnp.concatenate(
            [
                lax.dot_general(
                    feed_input, feed_grads, contract_first, preferred_element_type=jnp.float32
                ),
                lax.dot_general(
                    cotangent, hidden, contract_first, preferred_element_type=jnp.float32
                ),
            ],
            axis=1,
        ),
        "seq",
        scatter_dimension=0,
        tiled=True,
    )
    feed_gain_part = jnp.sum(normed_two * feed_in_grad, axis=0)
    scaled_two = feed_in_grad * piece_c.astype(jnp.float32)
    residual_grad = cotangent_f + factor_two * (
        scaled_two - normed_two * jnp.mean(normed_two * scaled_two, axis=-1, keepdims=True)
    )
    mixed_grad = residual_grad.astype(jnp.bfloat16)
    heads_grad = lax.dot_general(
        mixed_grad,
        lax.all_gather(output_weight, "seq", axis=0, tiled=True),
        contract_last,
        preferred_element_type=jnp.float32,
    ).reshape(heads_shape)
    head_gain_part = jnp.sum(unit_heads * heads_grad, axis=0).reshape(width)
    scaled_heads = heads_grad * head_gain_f
    out_back = (
        head_factor
        * (scaled_heads - unit_heads * jnp.mean(unit_heads * scaled_heads, axis=-1, keepdims=True))
    ).astype(jnp.bfloat16)
    output_backward_float = out_back.astype(jnp.float32)
    mixing_grad = plain_result("thd,shd->hts", out_back, value_rows)
    local_value = plain_result("hts,thd->shd", mixing_matrix, out_back)
    leading_value = precise_result("ixn,ixb->xnb", entry_point, output_backward_float)
    lifted_grad = growth_factor * precise_result(
        "ynf,fye->nye", mixing_grad * same[None], backward_pass
    ) + growth_factor * fresh_state[:, None, None] * precise_result(
        "egr,gjr->egj", output_backward_float, running_value_state
    )
    score_grad = probs * (lifted_grad - jnp.sum(probs * lifted_grad, axis=-1, keepdims=True))
    inner_grad = growth_factor * score_grad
    state_gradient = inner_grad * fresh_state[:, None, None]
    affinity_grad = (precise_result("thm,shm->hts", inner_grad, backward_pass) * same[None]).astype(
        jnp.bfloat16
    )
    leading_key = precise_result("ixn,ixb->xnb", state_gradient, query_float)
    back_state = jnp.concatenate([leading_key, leading_value], axis=-1)
    gain_out, later_grad = carried_in((carried_state, back_state), "seq", chain_join, (unit, blank))
    subsequent_key = later_grad[..., :head_size]
    subsequent_value = later_grad[..., head_size:]
    query_back = (
        (
            plain_result("via,avj->ivj", affinity_grad, key_rows)
            + precise_result("xfj,fjg->xfg", state_gradient, running_key_state)
        )
        .astype(jnp.bfloat16)
        .reshape(local_rows, width)
    )
    key_back = (
        (
            plain_result("hts,thd->shd", affinity_grad, query_rows)
            + precise_result("pzo,zot->pzt", weight_matrix, subsequent_key)
        )
        .astype(jnp.bfloat16)
        .reshape(local_rows, width)
    )
    value_back = (
        (local_value + precise_result("pzo,zot->pzt", weight_matrix, subsequent_value))
        .astype(jnp.bfloat16)
        .reshape(local_rows, width)
    )
    pieces = lax.all_gather((query_weight, key_weight, value_weight), "seq", axis=0, tiled=True)
    mixer_in_grad = (
        lax.dot_general(query_back, pieces[0], contract_last, preferred_element_type=jnp.float32)
        + lax.dot_general(key_back, pieces[1], contract_last, preferred_element_type=jnp.float32)
        + lax.dot_general(value_back, pieces[2], contract_last, preferred_element_type=jnp.float32)
    )
    mixer_gain_part = jnp.sum(normed_one * mixer_in_grad, axis=0)
    scaled_one = mixer_in_grad * piece_a.astype(jnp.float32)
    input_grad = residual_grad + factor_one * (
        scaled_one - normed_one * jnp.mean(normed_one * scaled_one, axis=-1, keepdims=True)
    )
    projection_grads = jnp.concatenate([query_back, key_back, value_back], axis=1)
    mixer_sums = lax.psum_scatter(
        jnp.concatenate(
            [
                lax.dot_general(
                    normed_b, projection_grads, contract_first, preferred_element_type=jnp.float32
                ),
                lax.dot_general(
                    normed_heads, mixed_grad, contract_first, preferred_element_type=jnp.float32
                ),
            ],
            axis=1,
        ),
        "seq",
        scatter_dimension=0,
        tiled=True,
    )
    gain_sums = (
        lax.psum_scatter(mixer_gain_part, "seq", scatter_dimension=0, tiled=True),
        lax.psum_scatter(head_gain_part, "seq", scatter_dimension=0, tiled=True),
        lax.psum_scatter(feed_gain_part, "seq", scatter_dimension=0, tiled=True),
    )
    return (
        block_out,
        input_grad,
        gain_sums[0],
        mixer_sums[:, :width],
        mixer_sums[:, width : 2 * width],
        mixer_sums[:, 2 * width : 3 * width],
        gain_sums[1],
        mixer_sums[:, 3 * width :],
        gain_sums[2],
        feed_sums[:, :hidden_width],
        feed_sums[:, hidden_width : 2 * hidden_width],
        feed_sums[:, 2 * hidden_width :],
    )


def solution(mesh):
    return jax.shard_map(
        local,
        mesh=mesh,
        in_specs=(
            P("seq", None),
            P("seq", None),
            P("seq", None),
            P(),
            P("seq"),
            P("seq", None),
            P("seq", None),
            P("seq", None),
            P("seq"),
            P("seq", None),
            P("seq"),
            P("seq", None),
            P("seq", None),
            P("seq", None),
        ),
        out_specs=(
            P("seq", None),
            P("seq", None),
            P("seq"),
            P("seq", None),
            P("seq", None),
            P("seq", None),
            P("seq"),
            P("seq", None),
            P("seq"),
            P("seq", None),
            P("seq", None),
            P("seq", None),
        ),
        check_vma=False,
    )
```

profile of v0, /device:TPU:14, one launch (start us, length us, event | category | flops | bytes accessed | tf_op | source)
XLA Modules:
  0.0 3828.9 jit_solution(6796610249351785658)
XLA Ops:
  21.5 41.1 %all-reduce.10 = (bf16[2048]{0:T(1024)(128)(2,1)S(1)}, bf16[2048]{0:T(1024)(128)(2,1)S(1)}, bf16[2048]{0:T(1024)(128)(2,1)S(1)}) all-reduce(bf16[2048]{0:T(1024)(128)(2,1)S(1)} %dynamic-update-slice, bf16[2048]{0:T(1024)(128)(2,1)S(1)} %dynamic-update-slice.1, bf16[2048]{0:T(1024)(128)(2,1)S(1)} %dynamic-update-slice.2), channel_id=1, replica_groups=mesh['seq'=32] {'seq'}, use_global_device_ids=true, to_apply=%add.2 | all-reduce | flops 6144 | bytes 24576
  62.9 25.9 all-gather.11.cloned.1.call-done
  94.2 73.6 %all-gather.15.cloned.1.call-done = bf16[2048,2048]{1,0:T(8,128)(2,1)} async-done(((bf16[64,2048]{1,0:T(8,128)(2,1)}), bf16[2048,2048]{1,0:T(8,128)(2,1)}) %all-gather.15.cloned.1.call-update) | async-done | bytes 8388624 | tf_op jit(solution)/shard_map/all_gather | solution.py:125
  177.2 29.9 all_gather.59
  207.2 39.6 %all-gather.13.cloned.1.call-done = bf16[2048,2048]{1,0:T(8,128)(2,1)} async-done(((bf16[64,2048]{1,0:T(8,128)(2,1)}), bf16[2048,2048]{1,0:T(8,128)(2,1)}) %all-gather.13.cloned.1.call-update) | async-done | bytes 8388624 | tf_op jit(solution)/shard_map/all_gather | solution.py:124
  255.5 186.1 %all-gather.27.cloned.1.call-done = f32[128,64,1024]{2,1,0:T(8,128)} async-done(((f32[4,64,1024]{2,1,0:T(8,128)}), f32[128,64,1024]{2,1,0:T(8,128)}) %all-gather.27.cloned.1.call-update) | async-done | bytes 33554448 | tf_op jit(solution)/shard_map/all_gather | solution.py:16
  441.5 48.4 %while.30 = (s32[]{:T(128)}, f32[4,64,1024]{2,1,0:T(8,128)S(1)}, s32[]{:T(128)}, f32[32,4,64]{2,1,0:T(4,128)S(1)}, f32[32,4,64,1024]{3,2,1,0:T(8,128)}, /*index=5*/s32[]{:T(128)}, s32[]{:T(128)}) while((s32[]{:T(128)}, f32[4,64,1024]{2,1,0:T(8,128)S(1)}, s32[]{:T(128)}, f32[32,4,64]{2,1,0:T(4,128)S(1)}, ...), condition=%wide.region_8.9_spmd.clone, body=%wide.region_7.8_spmd.clone.sunk | while | flops 1048580 | bytes 3148913 | solution.py:28
  503.7 18.1 all-gather.17.cloned.1.call-done
  527.3 138.7 %all-gather.19.cloned.1.call-done = bf16[2048,5632]{1,0:T(8,128)(2,1)} async-done(((bf16[64,5632]{1,0:T(8,128)(2,1)}), bf16[2048,5632]{1,0:T(8,128)(2,1)}) %all-gather.19.cloned.1.call-update) | async-done | bytes 23068688 | tf_op jit(solution)/shard_map/all_gather | solution.py:179
  666.0 11.5 fusion.106
  677.5 134.2 %all-gather.21.cloned.1.call-done = bf16[2048,5632]{1,0:T(8,128)(2,1)} async-done(((bf16[64,5632]{1,0:T(8,128)(2,1)}), bf16[2048,5632]{1,0:T(8,128)(2,1)}) %all-gather.21.cloned.1.call-update) | async-done | bytes 23068688 | tf_op jit(solution)/shard_map/all_gather | solution.py:180
  811.7 11.5 fusion.107
  823.2 134.1 %all-gather.23.cloned.1.call-done = bf16[2048,5632]{1,0:T(8,128)(2,1)} async-done(((bf16[64,5632]{1,0:T(8,128)(2,1)}), bf16[2048,5632]{1,0:T(8,128)(2,1)}) %all-gather.23.cloned.1.call-update) | async-done | bytes 23068688 | tf_op jit(solution)/shard_map/all_gather | solution.py:190
  957.3 14.1 multiply_convert_fusion
  971.4 13.7 fusion.108
  985.2 14.3 multiply_reduce_fusion
  1013.5 9.2 broadcast_multiply_fusion
  1025.3 20.3 convolution_bitcast_fusion
  1045.6 33.8 fusion.4
  1079.4 89.9 %pad_maximum_fusion = f32[2048,16896]{1,0:T(8,128)} fusion(f32[2048,5632]{1,0:T(8,128)} %convolution_bitcast_fusion, f32[2048,11264]{1,0:T(8,128)} %fusion.4), kind=kLoop, calls=%fused_computation.8 | loop fusion | flops 34603008 | bytes 276824064 | tf_op jit(solution)/shard_map/concatenate | solution.py:209
  1170.0 32.4 all_gather.68
  1210.2 8.4 fusion.82
  1218.6 44.0 %while.31 = (s32[]{:T(128)}, f32[4,64,1024]{2,1,0:T(8,128)S(1)}, s32[]{:T(128)}, bf16[32,4,64]{2,1,0:T(4,128)(2,1)S(1)}, bf16[32,4,64,1024]{3,2,1,0:T(8,128)(2,1...) while((s32[]{:T(128)}, f32[4,64,1024]{2,1,0:T(8,128)S(1)}, s32[]{:T(128)}, ...), condition=%wide.region_17.18_spmd.clone, body=%wide.region_16.17_spmd.clone.sunk | while | flops 1310984 | bytes 2624175 | solution.py:52
  1269.4 22.3 fusion.10
  1291.7 44.9 %pad_maximum_fusion.1 = f32[2048,8192]{1,0:T(8,128)} fusion(f32[2048,2048]{1,0:T(8,128)} %fusion.82, f32[2048,6144]{1,0:T(8,128)} %fusion.10), kind=kLoop, calls=%fused_computation.9 | loop fusion | flops 16777216 | bytes 134217728 | tf_op jit(solution)/shard_map/concatenate | solution.py:296
  1337.3 7.7 fusion.110
  1344.9 13.7 fusion.9
  1358.6 7.0 convolution_add_fusion.3
  1365.6 8.1 fusion.29
  1373.7 52.3 %all-reduce.9 = (f32[2048]{0:T(1024)S(1)}, f32[2048]{0:T(1024)S(1)}, f32[2048]{0:T(1024)S(1)}) all-reduce(f32[2048]{0:T(1024)S(1)} %get-tuple-element.300, f32[2048]{0:T(1024)S(1)} %bitcast.223, f32[2048]{0:T(1024)S(1)} %copy-done.48), channel_id=3, replica_groups=mesh['seq'=32] {'seq'}, use_global_device_ids=true, to_apply=%region_20.21.clone | all-reduce | flops 6144 | bytes 49152
  1430.6 1676.0 %all-reduce.13.cloned.1.call-done = f32[2048,16896]{1,0:T(8,128)} async-done(((f32[2048,16896]{1,0:T(8,128)}), f32[2048,16896]{1,0:T(8,128)}) %all-reduce.13.cloned.1.call-update) | async-done | bytes 138412048
  3111.7 707.4 %reduce-scatter.2.cloned.1.call-done = f32[64,8192]{1,0:T(8,128)} async-done(((f32[2048,8192]{1,0:T(8,128)}), f32[64,8192]{1,0:T(8,128)}) %reduce-scatter.2.cloned.1.call-update) | async-done | bytes 2097168 | tf_op jit(solution)/shard_map/reduce_scatter | solution.py:295
  (357 shorter events, 191.1 us)
Async XLA Ops:
  7.2 81.7 %all-gather.11.cloned.1.call-start = ((), (), s32[]{:S(2)}) async-start(), calls=%async_computation.1 | async-start | bytes 8650752 | tf_op jit(solution)/shard_map/all_gather | solution.py:126
  7.9 159.9 %all-gather.15.cloned.1.call-start = ((), (), s32[]{:S(2)}) async-start(), calls=%async_computation.3 | async-start | bytes 8650752 | tf_op jit(solution)/shard_map/all_gather | solution.py:125
  8.7 238.1 %all-gather.13.cloned.1.call-start = ((), (), s32[]{:S(2)}) async-start(), calls=%async_computation.2 | async-start | bytes 8650752 | tf_op jit(solution)/shard_map/all_gather | solution.py:124
  9.4 432.1 %all-gather.27.cloned.1.call-start = ((), (), s32[]{:S(2)}) async-start(), calls=%async_computation.10 | async-start | bytes 34603008 | tf_op jit(solution)/shard_map/all_gather | solution.py:16
  18.1 44.6 %copy-start.8 = (bf16[160,2048]{1,0:T(8,128)(2,1)S(1)}, bf16[160,2048]{1,0:T(8,128)(2,1)}, u32[]{:S(2)}) copy-start(bf16[160,2048]{1,0:T(8,128)(2,1)} %param.18) | copy-start | bytes 1966084
  20.7 152.0 %copy-start.16 = (f32[160,4,64]{0,2,1:T(8,128)}, f32[160,4,64]{0,2,1:T(8,128)S(1)}, u32[]{:S(2)}) copy-start(f32[160,4,64]{0,2,1:T(8,128)S(1)} %copy.162) | copy-start | bytes 491524
  62.7 184.1 %copy-start.42 = (f32[2048]{0:T(1024)}, f32[2048]{0:T(1024)S(1)}, u32[]{:S(2)}) copy-start(f32[2048]{0:T(1024)S(1)} %convert_element_type.125) | copy-start | bytes 24580
  62.9 183.8 %copy-start.46 = (f32[160]{0:T(256)}, f32[160]{0:T(256)S(1)}, u32[]{:S(2)}) copy-start(f32[160]{0:T(256)S(1)} %add_rsqrt_fusion.2) | copy-start | bytes 1924
  93.8 405.9 %copy-start.23 = (bf16[160,2048]{1,0:T(8,128)(2,1)}, bf16[160,2048]{1,0:T(8,128)(2,1)S(1)}, u32[]{:S(2)}) copy-start(bf16[160,2048]{1,0:T(8,128)(2,1)S(1)} %convolution_convert_fusion.2) | copy-start | bytes 1966084
  174.3 347.5 %all-gather.17.cloned.1.call-start = ((), (), s32[]{:S(2)}) async-start(), calls=%async_computation.4 | async-start | bytes 8650752 | tf_op jit(solution)/shard_map/all_gather | solution.py:171
  174.9 491.1 %all-gather.19.cloned.1.call-start = ((), (), s32[]{:S(2)}) async-start(), calls=%async_computation.5 | async-start | bytes 23789568 | tf_op jit(solution)/shard_map/all_gather | solution.py:179
  175.4 636.2 %all-gather.21.cloned.1.call-start = ((), (), s32[]{:S(2)}) async-start(), calls=%async_computation.6 | async-start | bytes 23789568 | tf_op jit(solution)/shard_map/all_gather | solution.py:180
  176.2 781.1 %all-gather.23.cloned.1.call-start = ((), (), s32[]{:S(2)}) async-start(), calls=%async_computation.7 | async-start | bytes 23789568 | tf_op jit(solution)/shard_map/all_gather | solution.py:190
  176.9 1041.7 %all-gather.25.cloned.1.call-start = ((), (), s32[]{:S(2)}) async-start(), calls=%async_computation.8 | async-start | bytes 17301504 | tf_op jit(solution)/shard_map/all_gather | solution.py:34
  177.2 835.4 %copy-start.14 = (f32[160,4,64]{0,2,1:T(8,128)}, f32[160,4,64]{0,2,1:T(8,128)S(1)}, u32[]{:S(2)}) copy-start(f32[160,4,64]{0,2,1:T(8,128)S(1)} %copy.160) | copy-start | bytes 491524
  207.2 803.2 %copy-start.34 = (f32[160,160]{1,0:T(8,128)}, f32[160,160]{1,0:T(8,128)S(1)}, u32[]{:S(2)}) copy-start(f32[160,160]{1,0:T(8,128)S(1)} %fusion.89) | copy-start | bytes 307204
  251.8 238.2 %copy-start.20 = (bf16[160,2048]{1,0:T(8,128)(2,1)}, bf16[160,2048]{1,0:T(8,128)(2,1)S(1)}, u32[]{:S(2)}) copy-start(bf16[160,2048]{1,0:T(8,128)(2,1)S(1)} %convolution_convert_fusion.1) | copy-start | bytes 1966084
  490.0 519.6 %copy-start = (f32[4,64,1024]{2,1,0:T(8,128)}, f32[4,64,1024]{2,1,0:T(8,128)S(1)}, u32[]{:S(2)}) copy-start(f32[4,64,1024]{2,1,0:T(8,128)S(1)} %get-tuple-element.238) | copy-start | bytes 3145732
  527.1 472.4 %copy-start.2 = (f32[160,2048]{1,0:T(8,128)}, f32[160,2048]{1,0:T(8,128)S(1)}, u32[]{:S(2)}) copy-start(f32[160,2048]{1,0:T(8,128)S(1)} %get-tuple-element.352) | copy-start | bytes 3932164
  971.4 13.7 copy-start.40
  1013.5 10.3 copy-start.21
  1025.2 2081.3 %all-reduce.13.cloned.1.call-start = ((), (), s32[]{:S(2)}) async-start(), calls=%async_computation.11 | async-start | bytes 276824064
  1025.3 20.3 copy-start.12
  1169.3 33.1 copy-start.15
  1169.3 33.1 copy-start.35
  1169.4 33.1 copy-start.44
  1169.4 33.8 copy-start.33
  1169.4 2649.7 %reduce-scatter.2.cloned.1.call-start = ((), (), s32[]{:S(2)}) async-start(), calls=%async_computation.9 | async-start | bytes 69206016 | tf_op jit(solution)/shard_map/reduce_scatter | solution.py:295
  1218.6 44.0 %copy-start.17 = (f32[160,4,64]{0,2,1:T(8,128)S(1)}, f32[160,4,64]{0,2,1:T(8,128)}, u32[]{:S(2)}) copy-start(f32[160,4,64]{0,2,1:T(8,128)} %copy-done.16) | copy-start | bytes 491524
  1337.3 7.7 copy-start.3
  1344.9 13.7 copy-start.19
  1365.6 8.1 copy-start.48
  (33 other events, 76.5 us)
Sparse Core Ops, SparseCore 0:
  10.9 77.9 all-gather.10
  91.7 76.0 all-gather.14
  170.6 76.0 all-gather.12
  250.0 191.4 all-gather.26
  444.3 77.5 all-gather.16
  524.5 141.4 all-gather.18
  668.8 142.7 all-gather.20
  814.5 142.7 all-gather.22
  1025.3 113.6 all-gather.24
  1169.5 1936.9 all-reduce.12
  3108.9 710.1 reduce-scatter.1
where the time goes:
time: 3840 us; the launch traced here: 3830 us
  waiting for transfers between devices  3140 us (82%)
  other arithmetic  253 us (7%)
  matrix products  233 us (6%)
  blocking collectives  156 us (4%)
    unnamed x12, waiting for transfers between devices  1680 us
    reduce_scatter x1, waiting for transfers between devices, local(): lax.psum_scatter(jnp.concatenate([lax.dot_general(normed_b, projection_gr...  707 us
    all_gather x1, waiting for transfers between devices, entering(): everything = jax.tree.map(lambda part: lax.all_gather(part, axis), shard)  186 us
    all_gather x1, waiting for transfers between devices, local(): lax.all_gather(gate_weight, 'seq', axis=0, tiled=True)  139 us
    all_gather x1, waiting for transfers between devices, local(): lax.all_gather(up_weight, 'seq', axis=0, tiled=True)  134 us
    all_gather x1, waiting for transfers between devices, local(): lax.all_gather(down_weight, 'seq', axis=0, tiled=True)  134 us
    unnamed x2, blocking collectives  93.5 us
    concatenate x1, other arithmetic, local(): jnp.concatenate([lax.dot_general(feed_input, feed_grads, contract_first,...  89.9 us
  transfers between devices with their start and end apart: 11, of which 10 were waited for; matrix products, arithmetic and copies ran while one was open for 11% of the time, Pallas kernels for 0%

commit v1 on v0

--- a/solution.py
+++ b/solution.py
@@ -121,8 +121,12 @@
     piece_a = lax.all_gather(mixer_gain, "seq", axis=0, tiled=True)
     piece_b = lax.all_gather(head_gain, "seq", axis=0, tiled=True)
     piece_c = lax.all_gather(feed_gain, "seq", axis=0, tiled=True)
-    piece_query = lax.all_gather(query_weight, "seq", axis=0, tiled=True)
-    piece_key = lax.all_gather(key_weight, "seq", axis=0, tiled=True)
+    recast_matrix = lambda xs, w_in: jnp.split(
+        lax.all_gather(jnp.concatenate([xs, w_in], axis=1), "seq", axis=0, tiled=True),
+        [xs.shape[1]],
+        axis=1,
+    )
+    piece_query, piece_key = recast_matrix(query_weight, key_weight)
     piece_value = lax.all_gather(value_weight, "seq", axis=0, tiled=True)
     section = (normed_one * piece_a.astype(jnp.float32)[None, :]).astype(jnp.bfloat16)
     normed_b = section

time: 3840 us -> 3930 us (1.023)
  waiting for transfers between devices: 3140 us -> 3230 us
    unnamed x12 -> x13, waiting for transfers between devices: 1680 us -> 1810 us
    all_gather x2 -> x3, waiting for transfers between devices: 113 us -> 110 us  [the longest x1 110 us: local(): lax.all_gather(jnp.concatenate([xs, w_in], axis=1), 'seq', axis=0, tiled=...]
  transfers between devices with their start and end apart: 11 -> 12, of which waited for: 10 -> 9; matrix products, arithmetic and copies ran while one was open for 11% -> 11% of each run, Pallas kernels for 0% -> 0%
where the time goes in v1:
time: 3930 us; the launch traced here: 3920 us
  waiting for transfers between devices  3230 us (82%)
  other arithmetic  254 us (6%)
  matrix products  232 us (6%)
  blocking collectives  154 us (4%)
    unnamed x13, waiting for transfers between devices  1810 us
    reduce_scatter x1, waiting for transfers between devices, local(): lax.psum_scatter(jnp.concatenate([lax.dot_general(normed_b, projection_gr...  707 us
    all_gather x1, waiting for transfers between devices, entering(): everything = jax.tree.map(lambda part: lax.all_gather(part, axis), shard)  150 us
    all_gather x1, waiting for transfers between devices, local(): lax.all_gather(gate_weight, 'seq', axis=0, tiled=True)  139 us
    all_gather x1, waiting for transfers between devices, local(): lax.all_gather(down_weight, 'seq', axis=0, tiled=True)  134 us
    all_gather x1, waiting for transfers between devices, local(): lax.all_gather(up_weight, 'seq', axis=0, tiled=True)  134 us
    all_gather x1, waiting for transfers between devices, local(): lax.all_gather(jnp.concatenate([xs, w_in], axis=1), 'seq', axis=0, tiled=...  110 us
    unnamed x2, blocking collectives  92.1 us
  transfers between devices with their start and end apart: 12, of which 9 were waited for; matrix products, arithmetic and copies ran while one was open for 11% of the time, Pallas kernels for 0%

profile of v1, /device:TPU:14, one launch (start us, length us, event | category | flops | bytes accessed | tf_op | source)
XLA Modules:
  0.0 3921.4 jit_solution(3124647416362613008)
XLA Ops:
  19.7 40.9 %all-reduce.10 = (bf16[2048]{0:T(1024)(128)(2,1)S(1)}, bf16[2048]{0:T(1024)(128)(2,1)S(1)}, bf16[2048]{0:T(1024)(128)(2,1)S(1)}) all-reduce(bf16[2048]{0:T(1024)(128)(2,1)S(1)} %dynamic-update-slice, bf16[2048]{0:T(1024)(128)(2,1)S(1)} %dynamic-update-slice.1, bf16[2048]{0:T(1024)(128)(2,1)S(1)} %dynamic-update-slice.2), channel_id=1, replica_groups=mesh['seq'=32] {'seq'}, use_global_device_ids=true, to_apply=%add.2 | all-reduce | flops 6144 | bytes 24576
  60.9 27.7 all-gather.12.cloned.1.call-done
  94.0 110.4 %all-gather.14.cloned.1.call-done = bf16[2048,4096]{1,0:T(8,128)(2,1)} async-done(((bf16[64,4096]{1,0:T(8,128)(2,1)}), bf16[2048,4096]{1,0:T(8,128)(2,1)}) %all-gather.14.cloned.1.call-update) | async-done | bytes 16777232 | tf_op jit(solution)/shard_map/all_gather | solution.py:125
  213.7 30.9 all_gather.59
  253.5 150.0 %all-gather.30.cloned.1.call-done = f32[128,64,1024]{2,1,0:T(8,128)} async-done(((f32[4,64,1024]{2,1,0:T(8,128)}), f32[128,64,1024]{2,1,0:T(8,128)}) %all-gather.30.cloned.1.call-update) | async-done | bytes 33554448 | tf_op jit(solution)/shard_map/all_gather | solution.py:16
  403.4 48.4 %while.30 = (s32[]{:T(128)}, f32[4,64,1024]{2,1,0:T(8,128)S(1)}, s32[]{:T(128)}, f32[32,4,64]{2,1,0:T(4,128)S(1)}, f32[32,4,64,1024]{3,2,1,0:T(8,128)}, /*index=5*/s32[]{:T(128)}, s32[]{:T(128)}) while((s32[]{:T(128)}, f32[4,64,1024]{2,1,0:T(8,128)S(1)}, s32[]{:T(128)}, f32[32,4,64]{2,1,0:T(4,128)S(1)}, ...), condition=%wide.region_8.9_spmd.clone, body=%wide.region_7.8_spmd.clone.sunk | while | flops 1048580 | bytes 3148913 | solution.py:28
  465.6 18.1 all-gather.16.cloned.1.call-done
  489.2 138.7 %all-gather.18.cloned.1.call-done = bf16[2048,5632]{1,0:T(8,128)(2,1)} async-done(((bf16[64,5632]{1,0:T(8,128)(2,1)}), bf16[2048,5632]{1,0:T(8,128)(2,1)}) %all-gather.18.cloned.1.call-update) | async-done | bytes 23068688 | tf_op jit(solution)/shard_map/all_gather | solution.py:183
  627.9 11.4 fusion.116
  639.3 134.1 %all-gather.20.cloned.1.call-done = bf16[2048,5632]{1,0:T(8,128)(2,1)} async-done(((bf16[64,5632]{1,0:T(8,128)(2,1)}), bf16[2048,5632]{1,0:T(8,128)(2,1)}) %all-gather.20.cloned.1.call-update) | async-done | bytes 23068688 | tf_op jit(solution)/shard_map/all_gather | solution.py:184
  773.4 11.5 fusion.117
  784.9 134.2 %all-gather.22.cloned.1.call-done = bf16[2048,5632]{1,0:T(8,128)(2,1)} async-done(((bf16[64,5632]{1,0:T(8,128)(2,1)}), bf16[2048,5632]{1,0:T(8,128)(2,1)}) %all-gather.22.cloned.1.call-update) | async-done | bytes 23068688 | tf_op jit(solution)/shard_map/all_gather | solution.py:194
  919.1 14.1 multiply_convert_fusion
  933.1 13.7 fusion.118
  946.9 14.3 multiply_reduce_fusion
  963.1 6.8 fusion.94
  975.3 9.2 broadcast_multiply_fusion
  988.3 20.2 convolution_bitcast_fusion
  1008.5 33.8 fusion.8
  1042.3 90.3 %pad_maximum_fusion = f32[2048,16896]{1,0:T(8,128)} fusion(f32[2048,5632]{1,0:T(8,128)} %convolution_bitcast_fusion, f32[2048,11264]{1,0:T(8,128)} %fusion.8), kind=kLoop, calls=%fused_computation.8 | loop fusion | flops 34603008 | bytes 276824064 | tf_op jit(solution)/shard_map/concatenate | solution.py:213
  1133.2 30.8 all_gather.69
  1171.9 8.4 fusion.92
  1180.3 43.6 %while.31 = (s32[]{:T(128)}, f32[4,64,1024]{2,1,0:T(8,128)S(1)}, s32[]{:T(128)}, bf16[32,4,64]{2,1,0:T(4,128)(2,1)S(1)}, bf16[32,4,64,1024]{3,2,1,0:T(8,128)(2,1...) while((s32[]{:T(128)}, f32[4,64,1024]{2,1,0:T(8,128)S(1)}, s32[]{:T(128)}, ...), condition=%wide.region_17.18_spmd.clone, body=%wide.region_16.17_spmd.clone.sunk | while | flops 1310984 | bytes 2624175 | solution.py:52
  1230.8 21.1 fusion.20
  1252.0 45.6 %pad_maximum_fusion.1 = f32[2048,8192]{1,0:T(8,128)} fusion(f32[2048,2048]{1,0:T(8,128)} %fusion.92, f32[2048,6144]{1,0:T(8,128)} %fusion.20), kind=kLoop, calls=%fused_computation.9 | loop fusion | flops 16777216 | bytes 134217728 | tf_op jit(solution)/shard_map/concatenate | solution.py:300
  1298.3 7.8 fusion.120
  1306.0 13.7 fusion.19
  1319.8 7.5 convolution_add_fusion.3
  1327.4 7.6 fusion.39
  1335.0 51.2 %all-reduce.9 = (f32[2048]{0:T(1024)S(1)}, f32[2048]{0:T(1024)S(1)}, f32[2048]{0:T(1024)S(1)}) all-reduce(f32[2048]{0:T(1024)S(1)} %get-tuple-element.300, f32[2048]{0:T(1024)S(1)} %bitcast.221, f32[2048]{0:T(1024)S(1)} %copy-done.50), channel_id=3, replica_groups=mesh['seq'=32] {'seq'}, use_global_device_ids=true, to_apply=%region_20.21.clone | all-reduce | flops 6144 | bytes 49152
  1390.7 1808.2 %all-reduce.13.cloned.1.call-done = f32[2048,16896]{1,0:T(8,128)} async-done(((f32[2048,16896]{1,0:T(8,128)}), f32[2048,16896]{1,0:T(8,128)}) %all-reduce.13.cloned.1.call-update) | async-done | bytes 138412048
  3204.0 707.2 %reduce-scatter.2.cloned.1.call-done = f32[64,8192]{1,0:T(8,128)} async-done(((f32[2048,8192]{1,0:T(8,128)}), f32[64,8192]{1,0:T(8,128)}) %reduce-scatter.2.cloned.1.call-update) | async-done | bytes 2097168 | tf_op jit(solution)/shard_map/reduce_scatter | solution.py:299
  (367 shorter events, 183.5 us)
Async XLA Ops:
  7.2 81.4 %all-gather.12.cloned.1.call-start = ((), (), s32[]{:S(2)}) async-start(), calls=%async_computation.1 | async-start | bytes 8650752 | tf_op jit(solution)/shard_map/all_gather | solution.py:130
  7.9 196.5 %all-gather.14.cloned.1.call-start = ((), (), s32[]{:S(2)}) async-start(), calls=%async_computation.2 | async-start | bytes 17301504 | tf_op jit(solution)/shard_map/all_gather | solution.py:125
  9.9 393.6 %all-gather.30.cloned.1.call-start = ((), (), s32[]{:S(2)}) async-start(), calls=%async_computation.11 | async-start | bytes 34603008 | tf_op jit(solution)/shard_map/all_gather | solution.py:16
  16.4 44.3 %copy-start.8 = (bf16[160,2048]{1,0:T(8,128)(2,1)S(1)}, bf16[160,2048]{1,0:T(8,128)(2,1)}, u32[]{:S(2)}) copy-start(bf16[160,2048]{1,0:T(8,128)(2,1)} %param.18) | copy-start | bytes 1966084
  18.9 190.4 %copy-start.16 = (f32[160,4,64]{0,2,1:T(8,128)}, f32[160,4,64]{0,2,1:T(8,128)S(1)}, u32[]{:S(2)}) copy-start(f32[160,4,64]{0,2,1:T(8,128)S(1)} %copy.162) | copy-start | bytes 491524
  60.7 184.0 %copy-start.43 = (f32[2048]{0:T(1024)}, f32[2048]{0:T(1024)S(1)}, u32[]{:S(2)}) copy-start(f32[2048]{0:T(1024)S(1)} %convert_element_type.125) | copy-start | bytes 24580
  60.9 183.7 %copy-start.48 = (f32[160]{0:T(256)}, f32[160]{0:T(256)S(1)}, u32[]{:S(2)}) copy-start(f32[160]{0:T(256)S(1)} %add_rsqrt_fusion.2) | copy-start | bytes 1924
  93.5 368.1 %copy-start.24 = (bf16[160,2048]{1,0:T(8,128)(2,1)}, bf16[160,2048]{1,0:T(8,128)(2,1)S(1)}, u32[]{:S(2)}) copy-start(bf16[160,2048]{1,0:T(8,128)(2,1)S(1)} %convolution_convert_fusion) | copy-start | bytes 1966084
  210.9 272.8 %all-gather.16.cloned.1.call-start = ((), (), s32[]{:S(2)}) async-start(), calls=%async_computation.3 | async-start | bytes 8650752 | tf_op jit(solution)/shard_map/all_gather | solution.py:175
  211.5 416.4 %all-gather.18.cloned.1.call-start = ((), (), s32[]{:S(2)}) async-start(), calls=%async_computation.4 | async-start | bytes 23789568 | tf_op jit(solution)/shard_map/all_gather | solution.py:183
  212.0 561.4 %all-gather.20.cloned.1.call-start = ((), (), s32[]{:S(2)}) async-start(), calls=%async_computation.5 | async-start | bytes 23789568 | tf_op jit(solution)/shard_map/all_gather | solution.py:184
  212.6 706.4 %all-gather.22.cloned.1.call-start = ((), (), s32[]{:S(2)}) async-start(), calls=%async_computation.6 | async-start | bytes 23789568 | tf_op jit(solution)/shard_map/all_gather | solution.py:194
  213.4 966.9 %all-gather.26.cloned.1.call-start = ((), (), s32[]{:S(2)}) async-start(), calls=%async_computation.8 | async-start | bytes 17301504 | tf_op jit(solution)/shard_map/all_gather | solution.py:34
  213.6 760.6 %copy-start.14 = (f32[160,4,64]{0,2,1:T(8,128)}, f32[160,4,64]{0,2,1:T(8,128)S(1)}, u32[]{:S(2)}) copy-start(f32[160,4,64]{0,2,1:T(8,128)S(1)} %copy.160) | copy-start | bytes 491524
  244.7 727.5 %copy-start.35 = (f32[160,160]{1,0:T(8,128)}, f32[160,160]{1,0:T(8,128)S(1)}, u32[]{:S(2)}) copy-start(f32[160,160]{1,0:T(8,128)S(1)} %fusion.99) | copy-start | bytes 307204
  249.7 202.2 %copy-start.21 = (bf16[160,2048]{1,0:T(8,128)(2,1)}, bf16[160,2048]{1,0:T(8,128)(2,1)S(1)}, u32[]{:S(2)}) copy-start(bf16[160,2048]{1,0:T(8,128)(2,1)S(1)} %fusion.13) | copy-start | bytes 1966084
  451.9 519.4 %copy-start = (f32[4,64,1024]{2,1,0:T(8,128)}, f32[4,64,1024]{2,1,0:T(8,128)S(1)}, u32[]{:S(2)}) copy-start(f32[4,64,1024]{2,1,0:T(8,128)S(1)} %get-tuple-element.238) | copy-start | bytes 3145732
  489.0 472.2 %copy-start.2 = (f32[160,2048]{1,0:T(8,128)}, f32[160,2048]{1,0:T(8,128)S(1)}, u32[]{:S(2)}) copy-start(f32[160,2048]{1,0:T(8,128)S(1)} %get-tuple-element.352) | copy-start | bytes 3932164
  933.1 13.7 copy-start.41
  975.2 10.3 copy-start.22
  986.9 311.3 %all-gather.24.cloned.1.call-start = ((), (), s32[]{:S(2)}) async-start(), calls=%async_computation.7 | async-start | bytes 8650752 | tf_op jit(solution)/shard_map/all_gather | solution.py:287
  987.7 332.2 %all-gather.28.cloned.1.call-start = ((), (), s32[]{:S(2)}) async-start(), calls=%async_computation.9 | async-start | bytes 8650752 | tf_op jit(solution)/shard_map/all_gather | solution.py:287
  988.2 2210.6 %all-reduce.13.cloned.1.call-start = ((), (), s32[]{:S(2)}) async-start(), calls=%async_computation.12 | async-start | bytes 276824064
  988.3 20.2 copy-start.12
  1132.6 31.4 copy-start.15
  1132.6 31.4 copy-start.36
  1132.6 31.4 copy-start.45
  1132.7 32.0 copy-start.34
  1132.7 2778.6 %reduce-scatter.2.cloned.1.call-start = ((), (), s32[]{:S(2)}) async-start(), calls=%async_computation.10 | async-start | bytes 69206016 | tf_op jit(solution)/shard_map/reduce_scatter | solution.py:299
  1180.3 43.6 %copy-start.17 = (f32[160,4,64]{0,2,1:T(8,128)S(1)}, f32[160,4,64]{0,2,1:T(8,128)}, u32[]{:S(2)}) copy-start(f32[160,4,64]{0,2,1:T(8,128)} %copy-done.16) | copy-start | bytes 491524
  1229.4 22.6 copy-start.19
  1298.3 7.8 copy-start.3
  (37 other events, 97.3 us)
Sparse Core Ops, SparseCore 0:
  10.9 77.6 all-gather.11
  92.0 112.3 all-gather.13
  211.0 192.4 all-gather.29
  406.2 77.5 all-gather.15
  486.4 141.4 all-gather.17
  630.6 142.7 all-gather.19
  776.2 142.7 all-gather.21
  987.0 113.6 all-gather.25
  1103.6 76.8 all-gather.23
  1183.2 76.0 all-gather.27
  1265.7 1933.0 all-reduce.12
  3201.1 710.1 reduce-scatter.1
